TPU v7x, 32 devices: a whole 2x2x4 slice. The times are simulated.
32 devices in a mesh: rec: 2 (over y), gx: 16 (over z, x, core).
Axes of the slice: x: 2, y: 2, z: 4, core: 2. Of those that a mesh axis runs over, the one named last changes fastest.
Arguments:
- velocity: float32 [4, 3, 96, 16, 128], P(None, None, ('rec', 'gx')), parts along dimension 2, may hold values from -6 to 36, as said below
- span_rim: float32 [4, 2, 96, 10, 6], P(None, None, ('rec', 'gx')), parts along dimension 2, may hold values from -6 to 36, as said below
- sketch_old: bfloat16 [3, 96, 10, 128, 256], P(None, ('rec', 'gx')), parts along dimension 1, as said below
- omega: float32 [4, 256], replicated, may hold values from -6 to 6
Outputs:
- basis: bfloat16 [3, 96, 10, 128, 256], P(None, ('rec', 'gx')), parts along dimension 1
- factor: float32 [512, 256], P('rec'), parts along dimension 0
There are 2 independent parts, one for each index of `rec`. A program takes and returns all parts, laid end to end along the dimension named above; an argument that names none is the same for every part. Nothing has to cross between parts.
Inputs may be any that keep to these rules, and one draw needn't show every extreme that they name: `sketch_old`: finite values of order one; rows differ in scale. `velocity`: finite values. `span_rim`: finite values.
All inputs are finite; a program needn't handle non-finite values.
Results may differ from a plain program's by a relative error of at most 0.014.
The roundings to bfloat16 on the way count: a program that leaves them out, or rounds other values in their place, can miss the bound.
Values sent between devices are 32-bit elements; how exact they have to be, the bound alone decides.
No kernel may reach another device: no remote copies, remote signals or barrier semaphores. Data moves between devices by JAX's collectives and lax.ppermute only.
A program may use at most 64 MiB of HBM per device.

v0:
```python
import jax
import jax.numpy as jnp
from jax import lax
from jax.sharding import PartitionSpec as P

COEFS = (0.75, -0.15, 1.0 / 60.0)


def extended_2(cells, sides, width):
    for axis, dim in sides:
        count = lax.axis_size(axis)
        head = lax.slice_in_dim(cells, 0, width, axis=dim)
        tail = lax.slice_in_dim(cells, cells.shape[dim] - width, cells.shape[dim], axis=dim)
        cells = jnp.concatenate(
            [
                lax.ppermute(tail, axis, [(i, (i + 1) % count) for i in range(count)]),
                cells,
                lax.ppermute(head, axis, [((i + 1) % count, i) for i in range(count)]),
            ],
            axis=dim,
        )
    return cells


def band_diff(padded, axis, count):
    out_shape = list(padded.shape)
    out_shape[axis] = count
    total = jnp.zeros(tuple(out_shape), jnp.float32)
    for shift_k, weight in zip((1, 2, 3), COEFS):
        ahead = lax.slice_in_dim(padded, 3 + shift_k, 3 + shift_k + count, axis=axis)
        behind = lax.slice_in_dim(padded, 3 - shift_k, 3 - shift_k + count, axis=axis)
        total = total + weight * (ahead - behind)
    return total


def span_extend(field, rim_part):
    return jnp.concatenate([rim_part[..., :3], field, rim_part[..., 3:]], axis=-1)


def upper_factor(gram):
    order = gram.shape[0]
    index = jnp.arange(order, dtype=jnp.int32)

    def column_step(j, lower):
        pick = (index == j).astype(gram.dtype)
        row = jnp.dot(pick, lower, precision=lax.Precision.HIGHEST)
        column = jnp.dot(gram, pick, precision=lax.Precision.HIGHEST) - jnp.dot(
            lower, row, precision=lax.Precision.HIGHEST
        )
        pivot = jnp.sqrt(jnp.sum(column * pick))
        below = (index > j).astype(gram.dtype)
        fresh = column * below / pivot + pick * pivot
        return lower + fresh[:, None] * pick[None, :]

    lower = lax.fori_loop(0, order, column_step, jnp.zeros_like(gram))
    return lower.T


def inverse_upper(upper):
    order = upper.shape[0]
    index = jnp.arange(order, dtype=jnp.int32)
    lower = upper.T

    def row_step(j, solved):
        pick = (index == j).astype(upper.dtype)
        row = jnp.dot(pick, lower, precision=lax.Precision.HIGHEST)
        pivot = jnp.sum(row * pick)
        fresh = (pick - jnp.dot(row, solved, precision=lax.Precision.HIGHEST)) / pivot
        return solved + pick[:, None] * fresh[None, :]

    solved = lax.fori_loop(0, order, row_step, jnp.zeros_like(upper))
    return solved.T


def gram_of(matrix):
    return lax.dot_general(
        matrix, matrix, (((0,), (0,)), ((), ())), preferred_element_type=jnp.float32
    )


def local(velocity, span_rim, sketch_old, omega):
    slabs = velocity.shape[2]
    band_rows = velocity.shape[3] - 6
    span_cells = velocity.shape[4]
    extended = extended_2(velocity, (("gx", 2),), 3)
    v_ext = extended[:, 1, :, 3 : 3 + band_rows]
    w_ext = extended[:, 2, :, 3 : 3 + band_rows]
    band = velocity[:, :, :, 3 : 3 + band_rows]
    u_span = span_extend(band[:, 0], span_rim[:, 0])
    v_span = span_extend(band[:, 1], span_rim[:, 1])
    vort_x = band_diff(velocity[:, 2], 2, band_rows) - band_diff(v_span, 3, span_cells)
    vort_y = band_diff(u_span, 3, span_cells) - band_diff(w_ext, 1, slabs)
    vort_z = band_diff(v_ext, 1, slabs) - band_diff(velocity[:, 0], 2, band_rows)
    vort = jnp.stack([vort_x, vort_y, vort_z], axis=1)
    sketch = sketch_old.astype(jnp.float32)
    for snap in range(vort.shape[0]):
        sketch = sketch + vort[snap][..., None] * omega[snap]
    sketch = sketch.astype(jnp.bfloat16)
    matrix = sketch.reshape(-1, sketch.shape[-1])
    total = jnp.float32(matrix.shape[0] * lax.axis_size("gx"))
    local_gram = gram_of(matrix) / total
    factor = upper_factor(lax.psum(local_gram, "gx"))
    inverse_one = inverse_upper(factor).astype(jnp.bfloat16)
    basis = jnp.dot(matrix, inverse_one, preferred_element_type=jnp.float32).astype(jnp.bfloat16)
    return (basis.reshape(sketch.shape), factor)


def solution(mesh):
    in_specs = (
        P(None, None, ("rec", "gx"), None, None),
        P(None, None, ("rec", "gx"), None, None),
        P(None, ("rec", "gx"), None, None, None),
        P(),
    )
    out_specs = (P(None, ("rec", "gx"), None, None, None), P("rec", None))
    return jax.shard_map(local, mesh=mesh, in_specs=in_specs, out_specs=out_specs, check_vma=False)
```

profile of v0, /device:TPU:1, one launch (start us, length us, event | category | flops | bytes accessed | tf_op | source)
XLA Modules:
  0.0 1443.7 jit_solution(5448559899833227195)
XLA Ops:
  7.3 2.6 collective-permute-start
  14.8 2.3 collective-permute-done
  18.7 7.5 add_convert_fusion
  26.3 2.5 copy-done
  28.8 2.4 fusion.21
  31.3 91.8 %all-reduce.2.cloned.1.call-done = f32[256,256]{1,0:T(8,128)} async-done(((f32[256,256]{1,0:T(8,128)}), f32[256,256]{1,0:T(8,128)}) %all-reduce.2.cloned.1.call-update) | async-done | bytes 262160 | tf_op jit(solution)/shard_map/psum | solution.py:102
  123.1 829.0 %while.30 = (s32[]{:T(128)}, f32[256,256]{1,0:T(8,128)S(1)}, f32[256,256]{1,0:T(8,128)}, s32[]{:T(128)}, s32[]{:T(128)}) while((s32[]{:T(128)}, f32[256,256]{1,0:T(8,128)S(1)}, f32[256,256]{1,0:T(8,128)}, s32[]{:T(128)}, s32[]{:T(128)}) %tuple.85), condition=%wide.region_3.0_spmd.clone.clone, body=%wide.region_1.0_spmd.clone.clone.sunk | while | flops 2690306 | bytes 1324397 | solution.py:55
  139.5 1.2 fusion.114
  142.7 1.2 fusion.114
  146.0 1.2 fusion.114
  149.2 1.2 fusion.114
  152.4 1.2 fusion.114
  155.7 1.2 fusion.114
  158.9 1.2 fusion.114
  162.1 1.2 fusion.114
  165.4 1.2 fusion.114
  168.6 1.2 fusion.114
  171.9 1.2 fusion.114
  175.1 1.2 fusion.114
  178.3 1.2 fusion.114
  181.6 1.2 fusion.114
  184.8 1.2 fusion.114
  952.9 476.9 %while.29 = (s32[]{:T(128)}, f32[256,256]{1,0:T(8,128)S(1)}, f32[256,256]{1,0:T(8,128)S(1)}, s32[]{:T(128)}, s32[]{:T(128)}) while((s32[]{:T(128)}, f32[256,256]{1,0:T(8,128)S(1)}, f32[256,256]{1,0:T(8,128)S(1)}, s32[]{:T(128)}, s32[]{:T(128)}) %tuple.88), condition=%wide.region_6.0_spmd.clone, body=%wide.region_4.0_spmd.clone.sunk | while | flops 1837314 | bytes 1058916 | solution.py:71
  1429.9 7.0 convolution_convert_fusion
  (3855 shorter events, 1094.9 us)
Async XLA Ops:
  7.2 115.9 %all-reduce.2.cloned.1.call-start = ((), (), s32[]{:S(2)}) async-start(), calls=%async_computation | async-start | bytes 524288 | tf_op jit(solution)/shard_map/psum | solution.py:102
  7.2 10.9 collective-permute-start.1
  7.3 9.8 collective-permute-start
  14.8 3.9 copy-start.1
  26.3 2.5 copy-start
Sparse Core Ops, SparseCore 0:
  31.4 91.6 all-reduce.1
where the time goes:
time: 1470 us; the launch traced here: 1440 us
  other arithmetic  573 us (39%)
  matrix products  547 us (37%)
  loops' own time  201 us (14%)
  waiting for transfers between devices  94.1 us (6%)
    dot_general x256, matrix products, column_step(): jnp.dot(gram, pick, precision=lax.Precision.HIGHEST)  301 us
    another operation x1, loops' own time, upper_factor(): lower = lax.fori_loop(0, order, column_step, jnp.zeros_like(gram))  189 us
    div x256, other arithmetic, row_step(): (pick - jnp.dot(row, solved, precision=lax.Precision.HIGHEST)) / pivot  170 us
    reduce_sum x256, other arithmetic, column_step(): pivot = jnp.sqrt(jnp.sum(column * pick))  170 us
    reduce_sum x256, other arithmetic, row_step(): pivot = jnp.sum(row * pick)  162 us
    psum x1, waiting for transfers between devices, local(): factor = upper_factor(lax.psum(local_gram, 'gx'))  91.8 us
    dot_general x256, matrix products, column_step(): jnp.dot(lower, row, precision=lax.Precision.HIGHEST)  81.5 us
    dot_general x256, matrix products, column_step(): row = jnp.dot(pick, lower, precision=lax.Precision.HIGHEST)  53.6 us
  transfers between devices with their start and end apart: 3, of which 2 were waited for; matrix products, arithmetic and copies ran while one was open for 0% of the time, Pallas kernels for 0%

commit v1 on v0

--- a/solution.py
+++ b/solution.py
@@ -99,7 +99,7 @@
     matrix = sketch.reshape(-1, sketch.shape[-1])
     total = jnp.float32(matrix.shape[0] * lax.axis_size("gx"))
     local_gram = gram_of(matrix) / total
-    factor = upper_factor(lax.psum(local_gram, "gx"))
+    factor = upper_factor(jnp.sum(lax.all_gather(local_gram, "gx"), axis=0))
     inverse_one = inverse_upper(factor).astype(jnp.bfloat16)
     basis = jnp.dot(matrix, inverse_one, preferred_element_type=jnp.float32).astype(jnp.bfloat16)
     return (basis.reshape(sketch.shape), factor)

time: 1470 us -> 1190 us (0.81)
  matrix products: 547 us -> 304 us
  waiting for transfers between devices: 94.1 us -> 55.5 us
    dot_general x256, matrix products: 301 us -> 57.9 us  [column_step(): jnp.dot(gram, pick, precision=lax.Precision.HIGHEST)]
    psum x1 -> x0, waiting for transfers between devices: 91.8 us -> none  [local(): factor = upper_factor(lax.psum(local_gram, 'gx'))]
    all_gather x0 -> x1, waiting for transfers between devices: none -> 53.2 us  [local(): factor = upper_factor(jnp.sum(lax.all_gather(local_gram, 'gx'), axis=0))]
  transfers between devices with their start and end apart: 3 -> 3, of which waited for: 2 -> 2; matrix products, arithmetic and copies ran while one was open for 0% -> 1% of each run, Pallas kernels for 0% -> 0%
where the time goes in v1:
time: 1190 us; the launch traced here: 1160 us
  other arithmetic  575 us (48%)
  matrix products  304 us (26%)
  loops' own time  201 us (17%)
  waiting for transfers between devices  55.5 us (5%)
  between operations  14.2 us (1%)
  local copies, waits for them, and re-layouts  12.5 us (1%)
    another operation x1, loops' own time, upper_factor(): lower = lax.fori_loop(0, order, column_step, jnp.zeros_like(gram))  189 us
    div x256, other arithmetic, row_step(): (pick - jnp.dot(row, solved, precision=lax.Precision.HIGHEST)) / pivot  170 us
    reduce_sum x256, other arithmetic, column_step(): pivot = jnp.sqrt(jnp.sum(column * pick))  170 us
    reduce_sum x256, other arithmetic, row_step(): pivot = jnp.sum(row * pick)  162 us
    dot_general x256, matrix products, column_step(): jnp.dot(lower, row, precision=lax.Precision.HIGHEST)  81.5 us
    dot_general x256, matrix products, column_step(): jnp.dot(gram, pick, precision=lax.Precision.HIGHEST)  57.9 us
    dot_general x256, matrix products, column_step(): row = jnp.dot(pick, lower, precision=lax.Precision.HIGHEST)  53.6 us
    all_gather x1, waiting for transfers between devices, local(): factor = upper_factor(jnp.sum(lax.all_gather(local_gram, 'gx'), axis=0))  53.2 us
  transfers between devices with their start and end apart: 3, of which 2 were waited for; matrix products, arithmetic and copies ran while one was open for 1% of the time, Pallas kernels for 0%

profile of v1, /device:TPU:1, one launch (start us, length us, event | category | flops | bytes accessed | tf_op | source)
XLA Modules:
  0.0 1164.5 jit_solution(17872321920813216173)
XLA Ops:
  7.3 2.6 collective-permute-start
  9.9 1.0 slice_bitcast_fusion.5
  10.9 1.0 slice_bitcast_fusion.4
  11.9 1.0 fusion.73
  13.6 0.8 fusion.76
  14.8 2.3 collective-permute-done
  17.1 1.0 constant_dynamic-update-slice_fusion.1
  18.7 7.5 add_convert_fusion
  26.3 2.5 copy-done
  28.8 2.4 fusion.21
  31.3 53.2 %all-gather.3.cloned.1.call-done = f32[4096,256]{1,0:T(8,128)} async-done(((f32[256,256]{1,0:T(8,128)}), f32[4096,256]{1,0:T(8,128)}) %all-gather.3.cloned.1.call-update) | async-done | bytes 4194320 | tf_op jit(solution)/shard_map/all_gather | solution.py:102
  84.5 2.5 reduce_sum.35
  87.0 585.8 %while.30 = (s32[]{:T(128)}, f32[256,256]{1,0:T(8,128)S(1)}, f32[256,256]{1,0:T(8,128)S(1)}, s32[]{:T(128)}, s32[]{:T(128)}) while((s32[]{:T(128)}, f32[256,256]{1,0:T(8,128)S(1)}, f32[256,256]{1,0:T(8,128)S(1)}, s32[]{:T(128)}, s32[]{:T(128)}) %tuple.85), condition=%wide.region_3.0_spmd.clone.clone, body=%wide.region_1.0_spmd.clone.clone.sunk | while | flops 2690306 | bytes 1324397 | solution.py:55
  672.8 0.8 copy.29
  673.7 476.9 %while.29 = (s32[]{:T(128)}, f32[256,256]{1,0:T(8,128)S(1)}, f32[256,256]{1,0:T(8,128)S(1)}, s32[]{:T(128)}, s32[]{:T(128)}) while((s32[]{:T(128)}, f32[256,256]{1,0:T(8,128)S(1)}, f32[256,256]{1,0:T(8,128)S(1)}, s32[]{:T(128)}, s32[]{:T(128)}) %tuple.88), condition=%wide.region_6.0_spmd.clone, body=%wide.region_4.0_spmd.clone.sunk | while | flops 1837314 | bytes 1058916 | solution.py:71
  674.7 0.7 subtract_divide_fusion.2
  676.6 0.7 subtract_divide_fusion.2
  678.5 0.7 subtract_divide_fusion.2
  680.3 0.7 subtract_divide_fusion.2
  682.2 0.7 subtract_divide_fusion.2
  684.0 0.7 subtract_divide_fusion.2
  685.9 0.7 subtract_divide_fusion.2
  691.5 0.7 subtract_divide_fusion.2
  1150.6 7.0 convolution_convert_fusion
  (3856 shorter events, 858.4 us)
Async XLA Ops:
  7.2 77.4 %all-gather.3.cloned.1.call-start = ((), (), s32[]{:S(2)}) async-start(), calls=%async_computation | async-start | bytes 4456448 | tf_op jit(solution)/shard_map/all_gather | solution.py:102
  7.2 10.9 collective-permute-start.1
  7.3 9.8 collective-permute-start
  14.8 3.9 copy-start.1
  26.3 2.5 copy-start
Sparse Core Ops, SparseCore 0:
  31.4 53.0 all-gather.2
